TPU v7x, 256 devices: a whole 4x4x8 slice. The times are simulated.
256 devices in a mesh: row: 32 (over z, x_hi, core), col: 8 (over y, x_lo).
Axes of the slice: x: 4 (x_hi: 2, x_lo: 2; x = x_hi * 2 + x_lo), y: 4, z: 8, core: 2. Of those that a mesh axis runs over, the one named last changes fastest.
Arguments:
- s_matrix: bfloat16 [2, 16384, 32768], P(None, 'row', 'col'), may hold values from -0.046875 to 0.046875
- slab: bfloat16 [2, 32768, 384], P(None, ('col', 'row')), may hold values from -6 to 6
- beam_hkl: int32 [3, 32768], P(None, ('col', 'row')), may hold values from -24 to 24
Outputs:
- squared: bfloat16 [2, 16384, 384], P(None, 'row', 'col')
All inputs are finite; a program needn't handle non-finite values.
Results may differ from a plain program's by a relative error of at most 0.014.
Values may be sent and summed in bfloat16 or wider, within the bound.
A program may use at most 64 MiB of HBM per device.

v0:
```python
import jax
import jax.numpy as jnp
from jax import lax
from jax.sharding import PartitionSpec as P


def apply_phase(slab, beam_hkl):
    hkl_float = beam_hkl.astype(jnp.float32)
    angles = (
        0.61
        * (hkl_float[0] * hkl_float[0] + hkl_float[1] * hkl_float[1] + hkl_float[2] * hkl_float[2])
        + 0.29 * hkl_float[0]
        - 0.17 * hkl_float[1]
        + 0.43 * hkl_float[2]
    )
    cosine = jnp.cos(angles)[:, None]
    sine = jnp.sin(angles)[:, None]
    slab_real = slab[0].astype(jnp.float32)
    slab_imag = slab[1].astype(jnp.float32)
    phased_real = cosine * slab_real - sine * slab_imag
    phased_imag = cosine * slab_imag + sine * slab_real
    return jnp.stack([phased_real, phased_imag]).astype(jnp.bfloat16)


def per_device(s_matrix, slab, beam_hkl):
    phased = apply_phase(slab, beam_hkl)
    gathered = lax.all_gather(phased, "row", axis=1, tiled=True)
    s_real = s_matrix[0]
    s_imag = s_matrix[1]
    part_real = jnp.dot(s_real, gathered[0], preferred_element_type=jnp.float32) - jnp.dot(
        s_imag, gathered[1], preferred_element_type=jnp.float32
    )
    part_imag = jnp.dot(s_real, gathered[1], preferred_element_type=jnp.float32) + jnp.dot(
        s_imag, gathered[0], preferred_element_type=jnp.float32
    )
    totals = jnp.stack([part_real, part_imag])
    return lax.psum_scatter(totals.astype(jnp.bfloat16), "col", scatter_dimension=2, tiled=True)


def solution(mesh):
    placed = (P(None, "row", "col"), P(None, ("col", "row"), None), P(None, ("col", "row")))
    return jax.shard_map(
        per_device, mesh=mesh, in_specs=placed, out_specs=P(None, "row", "col"), check_vma=False
    )
```

profile of v0, /device:TPU:4, one launch (start us, length us, event | category | flops | bytes accessed | tf_op | source)
XLA Modules:
  0.0 166.7 jit_solution(7687445948443255985)
XLA Ops:
  6.5 0.0 all-gather.2.cloned.1.call-start
  6.5 0.7 convert_element_type.15
  7.2 0.1 cosine_bitcast_fusion
  7.3 1.1 fusion.31
  8.4 0.7 pad_maximum_fusion.1
  9.1 0.0 all-gather.2.cloned.1.call-update
  9.1 0.0 reduce-scatter.2.cloned.1.call-start
  9.2 95.0 %all-gather.2.cloned.1.call-done = bf16[2,4096,384]{2,1,0:T(8,128)(2,1)} async-done(((bf16[2,128,384]{2,1,0:T(8,128)(2,1)}), bf16[2,4096,384]{2,1,0:T(8,128)(2,1)}) %all-gather.2.cloned.1.call-update) | async-done | bytes 6291472 | tf_op jit(solution)/shard_map/all_gather | solution.py:27
  104.2 0.0 copy-start
  104.2 5.1 %fusion = f32[384,512]{1,0:T(8,128)S(1)} fusion(bf16[2,512,4096]{2,1,0:T(8,128)(2,1)} %param.3, bf16[2,4096,384]{2,1,0:T(8,128)(2,1)} %all-gather.2.cloned.1.call-done), kind=kOutput, calls=%fused_computation | convolution fusion | flops 1610612736 | bytes 8126464 | tf_op jit(solution)/shard_map/dot_general | solution.py:33
  109.3 0.4 copy-done
  109.7 0.0 copy-start.1
  109.7 3.9 %fusion.2 = f32[384,512]{1,0:T(8,128)S(1)} fusion(bf16[2,512,4096]{2,1,0:T(8,128)(2,1)S(1)} %copy-done, bf16[2,4096,384]{2,1,0:T(8,128)(2,1)} %all-gather.2.cloned.1.call-done), kind=kOutput, calls=%fused_computation.2 | convolution fusion | flops 1610612736 | bytes 8126464 | tf_op jit(solution)/shard_map/dot_general | solution.py:30
  113.7 0.0 copy-done.1
  113.7 1.8 %fusion.27 = bf16[1,512,384]{1,2,0:T(8,128)(2,1)S(1)} fusion(f32[384,512]{1,0:T(8,128)S(1)} %fusion, bf16[2,512,4096]{2,1,0:T(8,128)(2,1)S(1)} %copy-done, bf16[2,4096,384]{2,1,0:T(8,128)(2,1)S(1)} %copy-done.1), kind=kOutput, calls=%fused_computation.19 | convolution fusion | flops 1611005952 | bytes 8519680 | tf_op jit(solution)/shard_map/dot_general | solution.py:33
  115.5 1.8 %fusion.24 = bf16[1,512,384]{1,2,0:T(8,128)(2,1)S(1)} fusion(f32[384,512]{1,0:T(8,128)S(1)} %fusion.2, bf16[2,512,4096]{2,1,0:T(8,128)(2,1)S(1)} %copy-done, bf16[2,4096,384]{2,1,0:T(8,128)(2,1)S(1)} %copy-done.1), kind=kOutput, calls=%fused_computation.18 | convolution fusion | flops 1611005952 | bytes 8519680 | tf_op jit(solution)/shard_map/dot_general | solution.py:30
  117.4 1.0 pad_maximum_fusion
  118.3 0.0 reduce-scatter.2.cloned.1.call-update
  118.3 41.5 %reduce-scatter.2.cloned.1.call-done = bf16[2,512,48]{1,2,0:T(8,128)(2,1)} async-done(((bf16[2,512,384]{1,2,0:T(8,128)(2,1)}), bf16[2,512,48]{1,2,0:T(8,128)(2,1)}) %reduce-scatter.2.cloned.1.call-update) | async-done | bytes 98320 | tf_op jit(solution)/shard_map/reduce_scatter | solution.py:37
  (1 shorter events, 0.0 us)
Async XLA Ops:
  6.5 97.7 %all-gather.2.cloned.1.call-start = ((), (), s32[]{:S(2)}) async-start(), calls=%async_computation.1 | async-start | bytes 6488064 | tf_op jit(solution)/shard_map/all_gather | solution.py:27
  9.1 150.7 %reduce-scatter.2.cloned.1.call-start = ((), (), s32[]{:S(2)}) async-start(), calls=%async_computation.2 | async-start | bytes 884736 | tf_op jit(solution)/shard_map/reduce_scatter | solution.py:37
  104.2 5.5 %copy-start = (bf16[2,512,4096]{2,1,0:T(8,128)(2,1)S(1)}, bf16[2,512,4096]{2,1,0:T(8,128)(2,1)}, u32[]{:S(2)}) copy-start(bf16[2,512,4096]{2,1,0:T(8,128)(2,1)} %param.3) | copy-start | bytes 25165828
  109.7 3.9 %copy-start.1 = (bf16[2,4096,384]{2,1,0:T(8,128)(2,1)S(1)}, bf16[2,4096,384]{2,1,0:T(8,128)(2,1)}, u32[]{:S(2)}) copy-start(bf16[2,4096,384]{2,1,0:T(8,128)(2,1)} %all-gather.2.cloned.1.call-done) | copy-start | bytes 18874372
Sparse Core Ops, SparseCore 0:
  10.0 94.1 all-gather.1
  118.5 41.3 reduce-scatter.1
where the time goes:
time: 167 us
  waiting for transfers between devices  137 us (82%)
  between operations  13.5 us (8%)
  matrix products  12.7 us (8%)
  other arithmetic  3.46 us (2%)
    all_gather x1, waiting for transfers between devices, per_device(): gathered = lax.all_gather(phased, 'row', axis=1, tiled=True)  95 us
    reduce_scatter x1, waiting for transfers between devices, per_device(): lax.psum_scatter(totals.astype(jnp.bfloat16), 'col', scatter_dimension=2,...  41.5 us
    dot_general x1, matrix products, per_device(): jnp.dot(s_imag, gathered[0], preferred_element_type=jnp.float32)  5.11 us
    dot_general x1, matrix products, per_device(): jnp.dot(s_imag, gathered[1], preferred_element_type=jnp.float32)  3.93 us
  transfers between devices with their start and end apart: 2, of which 2 were waited for; matrix products, arithmetic and copies ran while one was open for 0% of the time, Pallas kernels for 0%

commit v1 on v0

v1 whole, which is shorter than its diff:
```python
import functools

import jax
import jax.numpy as jnp
from jax import lax
from jax.experimental import pallas as pl
from jax.experimental.pallas import tpu as pltpu
from jax.sharding import PartitionSpec as P

MESH = pl.DeviceIdType.MESH
PANELS = 3
OFFSETS = (0, 1, -1, 2, -2, 3, -3, 4)
WIRE = 1.37
CORE_WIRE = 0.2
LATENCY = {"zp": 1.7, "zm": 1.7, "x": 2.5, "c": 1.0}
BACKLOG = 1.0
COARSE = (
    ((0, 0), (0, 1), (0, -1), (1, 0)),
    ((0, 2), (0, -2), (1, 1), (1, -1)),
    ((0, 3), (0, -3), (1, 2), (1, -2)),
    ((0, 4), (1, 3), (1, -3), (1, 4)),
)
FINE = COARSE[:3] + (((0, 4),), ((1, 3), (1, -3)), ((1, 4),))
GROUPS = (COARSE, COARSE, FINE)


def arrivals(p):
    table = {(p, 1, 0, None): ("x", (p, 0, 0, None))}
    for s, link in ((1, "zm"), (-1, "zp")):
        near = 0 if s == 1 else 1
        for d in (1, 2, 3):
            table[(p, 0, s * d, None)] = (link, (p, 0, s * (d - 1), None))
        table[(p, 0, 4, near)] = (link, (p, 0, s * 3, near))
        table[(p, 1, s, None)] = (link, (p, 1, 0, None))
        table[(p, 1, 2 * s, 1 - near)] = (link, (p, 1, s, 1 - near))
        table[(p, 1, 2 * s, near)] = ("x", (p, 0, 2 * s, near))
        table[(p, 1, 3 * s, None)] = ("x", (p, 0, 3 * s, None))
        table[(p, 1, 4, near)] = ("x", (p, 0, 4, near))
    return table


def pieces(part):
    p, h, d, half = part
    split = (h, d) in ((0, 4), (1, 4), (1, 2), (1, -2))
    if not split:
        return [(p, h, d, None)]
    return [(p, h, d, half)] if half is not None else [(p, h, d, 0), (p, h, d, 1)]


def schedule():
    sends = []
    for p in range(PANELS):
        for dst, (link, src) in arrivals(p).items():
            sends.append((link, dst, src, WIRE * (1.0 if dst[3] is None else 0.5)))
        for h in (0, 1):
            for d in OFFSETS:
                sends.append(("c", (p, h, d, "c"), (p, h, d, None), CORE_WIRE))

    def depth(dst):
        if dst[3] == "c":
            return 0
        below = [depth(s[1]) for s in sends if s[0] != "c" and dst in pieces(s[2])]
        return 1 + max(below, default=0)

    rank = {s[1]: (s[1][0], -depth(s[1])) for s in sends}
    arrive = {(p, 0, 0, None): 0.0 for p in range(PANELS)}
    free = {link: 0.0 for link in LATENCY}
    products = [(p, g) for p in range(PANELS) for g in range(len(GROUPS[p]))]
    order, now = [], 0.0

    def here(part):
        return all(arrive.get(k, 1e9) <= now for k in pieces(part))

    while sends or products:
        moved = False
        for link in ("zm", "zp", "x", "c"):
            able = [s for s in sends if s[0] == link and here(s[2])]
            if able and (link == "c" or free[link] - now < BACKLOG):
                best = min(able, key=lambda s: rank[s[1]])
                free[link] = max(free[link], now) + best[3]
                arrive[best[1]] = free[link] + LATENCY[link]
                order.append(("send", best[1]))
                sends.remove(best)
                now += 0.03
                moved = True
        if moved:
            continue
        able = []
        for p, g in products:
            first = (p, g) == min(k for k in products if k[0] == p)
            blocks = GROUPS[p][g]
            if first and all(here((p, h, d, None)) and arrive.get((p, h, d, "c"), 1e9) <= now for h, d in blocks):
                able.append((p, g))
        if able:
            p, g = able[0]
            products.remove((p, g))
            order.append(("product", p, g))
            now += 0.1 + 0.19 * len(GROUPS[p][g])
            continue
        later = [a for a in arrive.values() if a > now]
        later += [f - BACKLOG + 1e-6 for f in free.values() if f - BACKLOG + 1e-6 > now]
        now = min(later)
    return order


def kernel(s_any, slab_any, hkl_any, out_ref, s_ref, slab_ref, hkl_ref, got, acc, part, ysum, yrecv, xsend, xrecv,
           s_sem, in_sem, send_sem, recv_sem, rs_send, rs_recv):
    row = lax.axis_index("row")
    col = lax.axis_index("col")
    z, xh, core = row // 4, (row // 2) % 2, row % 2
    y, xl = col // 2, col % 2
    peer = {
        "zp": ((z + 1) % 8 * 4 + xh * 2 + core, col),
        "zm": ((z + 7) % 8 * 4 + xh * 2 + core, col),
        "x": (z * 4 + (1 - xh) * 2 + core, col),
        "c": (z * 4 + xh * 2 + 1 - core, col),
        "y1": (row, (y + 1) % 4 * 2 + xl),
        "y2": (row, (y + 2) % 4 * 2 + xl),
        "y3": (row, (y + 3) % 4 * 2 + xl),
        "xn": (row, y * 2 + 1 - xl),
    }

    slab_copy = pltpu.make_async_copy(slab_any, slab_ref, in_sem.at[0])
    hkl_copy = pltpu.make_async_copy(hkl_any, hkl_ref, in_sem.at[1])
    s_copies = [pltpu.make_async_copy(s_any.at[i], s_ref.at[i], s_sem.at[i]) for i in range(2)]
    slab_copy.start()
    hkl_copy.start()
    for c in s_copies:
        c.start()

    barrier = pltpu.get_barrier_semaphore()
    for name in peer:
        pl.semaphore_signal(barrier, inc=1, device_id=peer[name], device_id_type=MESH)

    hkl_copy.wait()
    f = hkl_ref[...].astype(jnp.float32)
    h0, h1, h2 = f[0:1], f[1:2], f[2:3]
    angles = 0.61 * (h0 * h0 + h1 * h1 + h2 * h2) + 0.29 * h0 - 0.17 * h1 + 0.43 * h2
    cosine, sine = jnp.cos(angles), jnp.sin(angles)
    slab_copy.wait()
    re = jnp.transpose(slab_ref[0].astype(jnp.float32))
    im = jnp.transpose(slab_ref[1].astype(jnp.float32))
    phased = (
        (cosine * re - sine * im).astype(jnp.bfloat16),
        (cosine * im + sine * re).astype(jnp.bfloat16),
    )

    def slot(p, h, d, mine):
        return (p * 16 + h * 8 + OFFSETS.index(d)) * 2 + mine

    for p in range(PANELS):
        for o in range(8):
            for comp in range(2):
                at = o * 32 + comp * 16
                got[slot(p, 0, 0, 0), at:at + 16, :] = phased[comp][48 * o + 16 * p:48 * o + 16 * p + 16, :]

    table = {}
    for p in range(PANELS):
        table.update(arrivals(p))
        for h in (0, 1):
            for d in OFFSETS:
                table[(p, h, d, "c")] = ("c", (p, h, d, None))
    index = {dst: i for i, dst in enumerate(table)}

    def copy_to(dst):
        link, src = table[dst]
        half = dst[3]
        source = got.at[slot(*src[:3], 0)]
        target = got.at[slot(*dst[:3], 1 if half == "c" else 0)]
        if half in (0, 1):
            source = source.at[pl.ds(128 * half, 128)]
            target = target.at[pl.ds(128 * half, 128)]
        return pltpu.make_async_remote_copy(
            src_ref=source, dst_ref=target, send_sem=send_sem.at[index[dst]], recv_sem=recv_sem.at[index[dst]],
            device_id=peer[link], device_id_type=MESH,
        )

    seen = {(p, 0, 0, None) for p in range(PANELS)}

    def need(part_key):
        keys = [part_key] if part_key[3] == "c" else pieces(part_key)
        for k in keys:
            if k not in seen:
                seen.add(k)
                copy_to(k).wait_recv()

    def lhs_rhs(p, h, d, mine):
        block = got[slot(p, h, d, mine)]
        turned = jnp.concatenate(
            [t for o in range(8) for t in (-block[o * 32 + 16:o * 32 + 32], block[o * 32:o * 32 + 16])], axis=0
        )
        chip = (z + d + 8) % 8 * 2 + (xh if h == 0 else 1 - xh)
        beam = chip * 2 + (core if mine == 0 else 1 - core)
        columns = pl.ds(pl.multiple_of(beam * 128, 128), 128)
        return [block, turned], [s_ref[0, :, columns], s_ref[1, :, columns]]

    def product(p, g):
        left, right = [], []
        for h, d in GROUPS[p][g]:
            for mine in (0, 1):
                a, b = lhs_rhs(p, h, d, mine)
                left += a
                right += b
        return lax.dot_general(
            jnp.concatenate(left, axis=1), jnp.concatenate(right, axis=1), (((1,), (1,)), ((), ())),
            preferred_element_type=jnp.float32,
        )

    def y_copy(p, j):
        to = (y + j) % 4
        return pltpu.make_async_remote_copy(
            src_ref=part.at[p, pl.ds(pl.multiple_of(to * 64, 64), 64)], dst_ref=yrecv.at[p, j - 1],
            send_sem=rs_send.at[p * 4 + j - 1], recv_sem=rs_recv.at[p * 4 + j - 1],
            device_id=peer[f"y{j}"], device_id_type=MESH,
        )

    def x_copy(p):
        return pltpu.make_async_remote_copy(
            src_ref=xsend.at[p], dst_ref=xrecv.at[p], send_sem=rs_send.at[p * 4 + 3], recv_sem=rs_recv.at[p * 4 + 3],
            device_id=peer["xn"], device_id_type=MESH,
        )

    def scatter_y(p):
        for j in (2, 1, 3):
            y_copy(p, j).start()

    def scatter_x(p):
        for j in (2, 1, 3):
            y_copy(p, j).wait_recv()

        def total(which):
            rows = pl.ds(pl.multiple_of(which * 32, 32), 32)
            t = acc[p, pl.ds(pl.multiple_of(y * 64 + which * 32, 32), 32)]
            for j in range(3):
                t += yrecv[p, j, rows].astype(jnp.float32)
            return t

        xsend[p] = total(1 - xl).astype(jnp.bfloat16)
        x_copy(p).start()
        ysum[p] = total(xl)

    def finish(p):
        x_copy(p).wait_recv()
        t = (ysum[p] + xrecv[p].astype(jnp.float32)).astype(jnp.bfloat16)
        out_ref[0, 16 * p:16 * p + 16, :] = t[0:16]
        out_ref[1, 16 * p:16 * p + 16, :] = t[16:32]

    pl.semaphore_wait(barrier, len(peer))
    waiting = []
    loaded = False
    for step in schedule():
        if step[0] == "send":
            need(table[step[1]][1])
            copy_to(step[1]).start()
            continue
        _, p, g = step
        for h, d in GROUPS[p][g]:
            need((p, h, d, None))
            need((p, h, d, "c"))
        if not loaded:
            loaded = True
            for c in s_copies:
                c.wait()
        result = product(p, g)
        if g:
            result += acc[p]
        acc[p] = result
        if waiting and g == 1:
            scatter_x(waiting[0])
        if waiting and g == 2:
            finish(waiting.pop(0))
        if g == len(GROUPS[p]) - 1:
            part[p] = result.astype(jnp.bfloat16)
            scatter_y(p)
            waiting.append(p)
    for dst in table:
        copy_to(dst).wait_send()
    for p in waiting:
        scatter_x(p)
    for p in waiting:
        finish(p)
    for p in range(PANELS):
        for j in (1, 2, 3):
            y_copy(p, j).wait_send()
        x_copy(p).wait_send()


def per_device(s_matrix, slab, beam_hkl):
    rows = s_matrix.shape[1]
    n_copies = PANELS * (len(arrivals(0)) + 16)
    out = pl.pallas_call(
        kernel,
        out_shape=jax.ShapeDtypeStruct((2, 48, rows), jnp.bfloat16),
        in_specs=[pl.BlockSpec(memory_space=pl.ANY)] * 3,
        out_specs=pl.BlockSpec(memory_space=pltpu.VMEM),
        scratch_shapes=[
            pltpu.VMEM(s_matrix.shape, jnp.bfloat16),
            pltpu.VMEM(slab.shape, jnp.bfloat16),
            pltpu.VMEM(beam_hkl.shape, jnp.int32),
            pltpu.VMEM((PANELS * 32, 256, 128), jnp.bfloat16),
            pltpu.VMEM((PANELS, 256, rows), jnp.float32),
            pltpu.VMEM((PANELS, 256, rows), jnp.bfloat16),
            pltpu.VMEM((PANELS, 32, rows), jnp.float32),
            pltpu.VMEM((PANELS, 3, 64, rows), jnp.bfloat16),
            pltpu.VMEM((PANELS, 32, rows), jnp.bfloat16),
            pltpu.VMEM((PANELS, 32, rows), jnp.bfloat16),
            pltpu.SemaphoreType.DMA((2,)),
            pltpu.SemaphoreType.DMA((2,)),
            pltpu.SemaphoreType.DMA((n_copies,)),
            pltpu.SemaphoreType.DMA((n_copies,)),
            pltpu.SemaphoreType.DMA((PANELS * 4,)),
            pltpu.SemaphoreType.DMA((PANELS * 4,)),
        ],
        compiler_params=pltpu.CompilerParams(
            collective_id=0, has_side_effects=True, vmem_limit_bytes=48 * 2**20
        ),
        name="squared",
    )(s_matrix, slab, beam_hkl)
    return jnp.swapaxes(out, 1, 2)


def solution(mesh):
    placed = (P(None, "row", "col"), P(None, ("col", "row"), None), P(None, ("col", "row")))
    return jax.shard_map(
        per_device, mesh=mesh, in_specs=placed, out_specs=P(None, "row", "col"), check_vma=False
    )
```

time: 167 us -> 58 us (0.35)
  the two profiles are of different devices: /device:TPU:4 before, /device:TPU:1 now
where the time goes in v1:
time: 58 us; the launch traced here: 57.8 us
  Pallas kernels  55.6 us (96%)
  local copies, waits for them, and re-layouts  2.25 us (4%)
    pallas_call x1, Pallas kernels, per_device(): pl.pallas_call(kernel, out_shape=jax.ShapeDtypeStruct((2, 48, rows), jnp....  55.6 us
    unnamed x5, local copies, waits for them, and re-layouts  2.25 us

profile of v1, /device:TPU:1, one launch (start us, length us, event | category | flops | bytes accessed | tf_op | source)
XLA Modules:
  0.0 57.8 jit_solution(13949567408940583010)
XLA Ops:
  0.0 0.0 copy-start
  0.0 0.9 %copy-done = bf16[2,128,384]{2,1,0:T(8,128)(2,1)S(1)} copy-done((bf16[2,128,384]{2,1,0:T(8,128)(2,1)S(1)}, bf16[2,128,384]{2,1,0:T(8,128)(2,1)}, u32[]{:S(2)}) %copy-start) | copy-done | bytes 196632
  0.9 0.0 copy-start.1
  0.9 0.7 %copy-done.1 = s32[3,128]{1,0:T(4,128)S(1)} copy-done((s32[3,128]{1,0:T(4,128)S(1)}, s32[3,128]{1,0:T(4,128)}, u32[]{:S(2)}) %copy-start.1) | copy-done | bytes 1560
  1.6 55.6 %squared.1 = bf16[2,48,512]{2,1,0:T(8,128)(2,1)S(1)} custom-call(bf16[2,512,4096]{2,1,0:T(8,128)(2,1)} %s_any.1, bf16[2,128,384]{2,1,0:T(8,128)(2,1)S(1)} %copy-done, s32[3,128]{1,0:T(4,128)S(1)} %copy-done.1), custom_call_target="tpu_custom_call" | custom-call | tf_op jit(solution)/shard_map/squared/pallas_call | solution.py:291
  57.2 0.6 %copy.5 = bf16[2,512,48]{1,2,0:T(8,128)(2,1)} copy(bf16[2,512,48]{1,2,0:T(8,128)(2,1)S(1)} %bitcast.1) | data formatting | bytes 196608
Async XLA Ops:
  0.0 0.9 %copy-start = (bf16[2,128,384]{2,1,0:T(8,128)(2,1)S(1)}, bf16[2,128,384]{2,1,0:T(8,128)(2,1)}, u32[]{:S(2)}) copy-start(bf16[2,128,384]{2,1,0:T(8,128)(2,1)} %slab_any.1) | copy-start | bytes 589828
  0.9 0.7 %copy-start.1 = (s32[3,128]{1,0:T(4,128)S(1)}, s32[3,128]{1,0:T(4,128)}, u32[]{:S(2)}) copy-start(s32[3,128]{1,0:T(4,128)} %hkl_any.1) | copy-start | bytes 4612

commit v2 on v0

v2 whole, which is shorter than its diff:
```python
import jax
import jax.numpy as jnp
from jax import lax
from jax.experimental import pallas as pl
from jax.experimental.pallas import tpu as pltpu
from jax.sharding import PartitionSpec as P

MESH = pl.DeviceIdType.MESH
UNIT = 8
PANELS = ((0, 2), (2, 2), (4, 1), (5, 1))
DIRECT = (3,)
OFFSETS = (0, 1, -1, 2, -2, 3, -3, 4)
COARSE = (
    ((0, 0), (0, 1), (0, -1), (1, 0)),
    ((0, 2), (0, -2), (1, 1), (1, -1)),
    ((0, 3), (0, -3), (1, 2), (1, -2)),
    ((0, 4), (1, 3), (1, -3), (1, 4)),
)
FINE = COARSE[:3] + (((0, 4),), ((1, 3), (1, -3)), ((1, 4),))
GROUPS = (COARSE, COARSE, COARSE, FINE)

WIRE, CORE_WIRE = 0.69, 0.1
LATENCY = {"zm": 1.7, "zp": 1.7, "x": 2.5, "c": 1.0}
BACKLOG = 1.0


def arrivals(p):
    table = {(p, 1, 0, None): ("x", (p, 0, 0, None))}
    for s, link in ((1, "zm"), (-1, "zp")):
        near = 0 if s == 1 else 1
        for d in (1, 2, 3):
            table[(p, 0, s * d, None)] = (link, (p, 0, s * (d - 1), None))
        table[(p, 0, 4, near)] = (link, (p, 0, s * 3, near))
        table[(p, 1, s, None)] = ("x", (p, 0, s, None))
        table[(p, 1, 2 * s, None)] = (link, (p, 1, s, None))
        table[(p, 1, 3 * s, 1 - near)] = (link, (p, 1, 2 * s, 1 - near))
        table[(p, 1, 3 * s, near)] = ("x", (p, 0, 3 * s, near))
        table[(p, 1, 4, near)] = ("x", (p, 0, 4, near))
    return table


def copies():
    table = {}
    for p in range(len(PANELS)):
        table.update(arrivals(p))
        for h in (0, 1):
            for d in OFFSETS:
                table[(p, h, d, "c")] = ("c", (p, h, d, None))
    return table


def pieces(part, table):
    p, h, d, half = part
    if part in table or (h, d) == (0, 0):
        return [part]
    if half is None:
        return [(p, h, d, 0), (p, h, d, 1)]
    return pieces((p, h, d, None), table)


def schedule(table):
    sends = [(link, dst, pieces(src, table)) for dst, (link, src) in table.items()]

    def depth(dst):
        if dst[3] == "c":
            return 0
        return 1 + max([depth(s[1]) for s in sends if s[0] != "c" and dst in s[2]], default=0)

    rank = {s[1]: (s[1][0], -depth(s[1])) for s in sends}
    arrive = {(p, 0, 0, None): 0.0 for p in range(len(PANELS))}
    free = {link: 0.0 for link in LATENCY}
    products = [(p, g) for p in range(len(PANELS)) for g in range(len(GROUPS[p]))]
    later, order, now = [], [], 0.0
    while sends or products or later:
        moved = False
        for link in LATENCY:
            able = [s for s in sends if s[0] == link and all(arrive.get(k, 1e9) <= now for k in s[2])]
            if able and (link == "c" or free[link] - now < BACKLOG):
                best = min(able, key=lambda s: rank[s[1]])
                p, _, _, half = best[1]
                wire = PANELS[p][1] * (CORE_WIRE if link == "c" else WIRE * (1.0 if half is None else 0.5))
                free[link] = max(free[link], now) + wire
                arrive[best[1]] = free[link] + LATENCY[link]
                order.append(("send", best[1]))
                sends.remove(best)
                now += 0.03
                moved = True
        if moved:
            continue
        if later and later[0][0] <= now:
            _, op, p = later.pop(0)
            units = PANELS[p][1]
            order.append((op, p))
            now += 0.1 * units
            if op == "scatter_x":
                free["x"] = max(free["x"], now) + 0.35 * units
                later.append((free["x"] + 1.9, "finish", p))
                later.sort()
            continue
        if products:
            p, g = products[0]
            units = PANELS[p][1]
            parts = [k for h, d in GROUPS[p][g] for k in pieces((p, h, d, None), table) + [(p, h, d, "c")]]
            if all(arrive.get(k, 1e9) <= now for k in parts):
                products.pop(0)
                order.append(("product", p, g))
                now += 0.05 + (0.1 + 0.17 * len(GROUPS[p][g])) * units / 2
                if g == len(GROUPS[p]) - 1:
                    order.append(("scatter", p))
                    now += 0.1 * units
                    if p in DIRECT:
                        later.append((now + 1.35 * units + 3.4, "finish", p))
                    else:
                        later.append((now + 1.35 * units + 3.0, "scatter_x", p))
                    later.sort()
                continue
        events = list(arrive.values()) + [t[0] for t in later]
        events += [f - BACKLOG + 1e-6 for link, f in free.items() if any(s[0] == link for s in sends)]
        now = min(t for t in events if t > now)
    return order


def kernel(s_any, slab_any, hkl_any, out_ref, s_ref, slab_ref, hkl_ref, turned, got, acc, total, part, yrecv, drecv,
           ysum, xsend, xrecv, final, in_sem, send_sem, recv_sem, rs_send, rs_recv):
    row = lax.axis_index("row")
    col = lax.axis_index("col")
    z, xh, core = row // 4, (row // 2) % 2, row % 2
    y, xl = col // 2, col % 2
    rows = s_any.shape[1]
    peer = {
        "zp": ((z + 1) % 8 * 4 + xh * 2 + core, col),
        "zm": ((z + 7) % 8 * 4 + xh * 2 + core, col),
        "x": (z * 4 + (1 - xh) * 2 + core, col),
        "c": (z * 4 + xh * 2 + 1 - core, col),
    }
    owner = {(dy, dx): (y + dy) % 4 * 2 + (xl + dx) % 2 for dy in range(4) for dx in range(2) if dy or dx}
    owners = list(owner)
    for k in owner:
        peer[k] = (row, owner[k])

    slab_copy = pltpu.make_async_copy(slab_any, slab_ref, in_sem.at[0])
    hkl_copy = pltpu.make_async_copy(hkl_any, hkl_ref, in_sem.at[1])
    s_copies = [
        pltpu.make_async_copy(s_any.at[i], s_ref.at[pl.ds(i * rows, rows)], in_sem.at[2 + i]) for i in range(2)
    ]
    slab_copy.start()
    hkl_copy.start()
    barrier = pltpu.get_barrier_semaphore()
    for name in peer:
        pl.semaphore_signal(barrier, inc=1, device_id=peer[name], device_id_type=MESH)

    hkl_copy.wait()
    f = hkl_ref[...].astype(jnp.float32)
    h0, h1, h2 = f[0:1], f[1:2], f[2:3]
    angles = 0.61 * (h0 * h0 + h1 * h1 + h2 * h2) + 0.29 * h0 - 0.17 * h1 + 0.43 * h2
    cosine, sine = jnp.cos(angles), jnp.sin(angles)
    slab_copy.wait()
    for c in s_copies:
        c.start()
    for i in range(2):
        turned[i] = jnp.transpose(slab_ref[i].astype(jnp.float32))

    def slot(p, h, d, mine):
        first, units = PANELS[p]
        return first * 32 + ((h * 8 + OFFSETS.index(d)) * 2 + mine) * units

    def phase(p):
        first, units = PANELS[p]
        for u in range(units):
            for o in range(8):
                at = 48 * o + UNIT * (first + u)
                re, im = turned[0, at:at + UNIT], turned[1, at:at + UNIT]
                both = jnp.concatenate([cosine * re - sine * im, cosine * im + sine * re], axis=0)
                got[slot(p, 0, 0, 0) + u, 16 * o:16 * o + 16] = both.astype(jnp.bfloat16)

    table = copies()
    index = {dst: i for i, dst in enumerate(table)}

    def copy_to(dst):
        link, src = table[dst]
        half, units = dst[3], PANELS[dst[0]][1]

        def ref(part, mine):
            at = slot(*part[:3], mine)
            if half not in (0, 1):
                return got.at[pl.ds(at, units)]
            if units == 1:
                return got.at[at, pl.ds(64 * half, 64)]
            return got.at[pl.ds(at + half * units // 2, units // 2)]

        return pltpu.make_async_remote_copy(
            src_ref=ref(src, 0), dst_ref=ref(dst, 1 if half == "c" else 0),
            send_sem=send_sem.at[index[dst]], recv_sem=recv_sem.at[index[dst]],
            device_id=peer[link], device_id_type=MESH,
        )

    seen = set()

    def need(part_key):
        for k in pieces(part_key, table):
            if k in seen:
                continue
            seen.add(k)
            if k[1:] == (0, 0, None):
                phase(k[0])
            else:
                copy_to(k).wait_recv()

    def product(p, g):
        left, right = [], []
        units = PANELS[p][1]
        for h, d in GROUPS[p][g]:
            for mine in (0, 1):
                left.append(got[pl.ds(slot(p, h, d, mine), units)].reshape(units * 128, 128))
                chip = (z + d + 8) % 8 * 2 + (xh if h == 0 else 1 - xh)
                beam = chip * 2 + (core if mine == 0 else 1 - core)
                right.append(s_ref[:, pl.ds(pl.multiple_of(beam * 128, 128), 128)])
        result = lax.dot_general(
            jnp.concatenate(left, axis=1), jnp.concatenate(right, axis=1), (((1,), (1,)), ((), ())),
            preferred_element_type=jnp.float32,
        )
        size = pl.ds(0, units * 128)
        if g:
            result += acc[size]
        if g < len(GROUPS[p]) - 1:
            acc[size] = result
            return
        pairs = result.reshape(units * 8, 2, UNIT, 2 * rows)
        re, im = pairs[:, 0], pairs[:, 1]
        both = jnp.stack([re[..., :rows] - im[..., rows:], im[..., :rows] + re[..., rows:]], axis=1)
        both = both.reshape(units, 128, rows)
        mine = pl.ds(PANELS[p][0], units)
        total[mine] = both
        part[mine] = both.astype(jnp.bfloat16)

    def y_copy(p, j):
        to = (y + j) % 4
        mine = pl.ds(PANELS[p][0], PANELS[p][1])
        return pltpu.make_async_remote_copy(
            src_ref=part.at[mine, pl.ds(pl.multiple_of(to * 32, 32), 32)], dst_ref=yrecv.at[j - 1, mine],
            send_sem=rs_send.at[p * 8 + j], recv_sem=rs_recv.at[p * 8 + j],
            device_id=peer[(j, 0)], device_id_type=MESH,
        )

    def x_copy(p):
        mine = pl.ds(PANELS[p][0], PANELS[p][1])
        return pltpu.make_async_remote_copy(
            src_ref=xsend.at[mine], dst_ref=xrecv.at[mine], send_sem=rs_send.at[p * 8], recv_sem=rs_recv.at[p * 8],
            device_id=peer[(0, 1)], device_id_type=MESH,
        )

    def direct_copy(p, k):
        mine = pl.ds(PANELS[p][0], PANELS[p][1])
        i = owners.index(k)
        return pltpu.make_async_remote_copy(
            src_ref=part.at[mine, pl.ds(pl.multiple_of(owner[k] * 16, 16), 16)], dst_ref=drecv.at[i, mine],
            send_sem=rs_send.at[p * 8 + i], recv_sem=rs_recv.at[p * 8 + i],
            device_id=peer[k], device_id_type=MESH,
        )

    def scatter_copies(p):
        if p in DIRECT:
            return [direct_copy(p, k) for k in ((2, 1), (2, 0), (1, 1), (3, 1), (1, 0), (3, 0), (0, 1))]
        return [y_copy(p, j) for j in (2, 1, 3)]

    def scatter(p):
        for c in scatter_copies(p):
            c.start()

    def scatter_x(p):
        for c in scatter_copies(p):
            c.wait_recv()
        for u in range(PANELS[p][0], sum(PANELS[p])):
            for to in (1, 0):
                which = (xl + to) % 2
                t = total[u, pl.ds(pl.multiple_of(y * 32 + which * 16, 16), 16)]
                for j in range(3):
                    t += yrecv[j, u, pl.ds(pl.multiple_of(which * 16, 16), 16)].astype(jnp.float32)
                if to:
                    xsend[u] = t.astype(jnp.bfloat16)
                else:
                    ysum[u] = t
        x_copy(p).start()

    def finish(p):
        for c in scatter_copies(p) if p in DIRECT else [x_copy(p)]:
            c.wait_recv()
        for u in range(PANELS[p][0], sum(PANELS[p])):
            if p in DIRECT:
                t = total[u, pl.ds(pl.multiple_of(col * 16, 16), 16)]
                for i in range(len(owners)):
                    t += drecv[i, u].astype(jnp.float32)
            else:
                t = ysum[u] + xrecv[u].astype(jnp.float32)
            final[0, UNIT * u:UNIT * (u + 1)] = t[:UNIT]
            final[1, UNIT * u:UNIT * (u + 1)] = t[UNIT:]

    need((0, 0, 0, None))
    pl.semaphore_wait(barrier, len(peer))
    order = schedule(table)
    drained = max(i for i, step in enumerate(order) if step[0] == "scatter")
    loaded = False
    for i, step in enumerate(order):
        if step[0] == "send":
            need(table[step[1]][1])
            copy_to(step[1]).start()
        elif step[0] == "product":
            _, p, g = step
            for h, d in GROUPS[p][g]:
                need((p, h, d, None))
                need((p, h, d, "c"))
            if not loaded:
                loaded = True
                for c in s_copies:
                    c.wait()
            product(p, g)
        else:
            {"scatter": scatter, "scatter_x": scatter_x, "finish": finish}[step[0]](step[1])
        if i == drained:
            for dst in table:
                copy_to(dst).wait_send()
    out_ref[...] = final[...].astype(jnp.bfloat16)
    for p in range(len(PANELS)):
        for c in scatter_copies(p) + ([] if p in DIRECT else [x_copy(p)]):
            c.wait_send()


def per_device(s_matrix, slab, beam_hkl):
    rows, beams = s_matrix.shape[1:]
    units = sum(PANELS[-1])
    most = max(n for _, n in PANELS)
    n_copies = len(copies())
    out = pl.pallas_call(
        kernel,
        out_shape=jax.ShapeDtypeStruct((2, units * UNIT, rows), jnp.bfloat16),
        in_specs=[pl.BlockSpec(memory_space=pl.ANY)] * 3,
        out_specs=pl.BlockSpec(memory_space=pltpu.VMEM),
        scratch_shapes=[
            pltpu.VMEM((2 * rows, beams), jnp.bfloat16),
            pltpu.VMEM(slab.shape, jnp.bfloat16),
            pltpu.VMEM(beam_hkl.shape, jnp.int32),
            pltpu.VMEM((2, slab.shape[2], slab.shape[1]), jnp.float32),
            pltpu.VMEM((units * 32, 128, 128), jnp.bfloat16),
            pltpu.VMEM((most * 128, 2 * rows), jnp.float32),
            pltpu.VMEM((units, 128, rows), jnp.float32),
            pltpu.VMEM((units, 128, rows), jnp.bfloat16),
            pltpu.VMEM((3, units, 32, rows), jnp.bfloat16),
            pltpu.VMEM((7, units, 16, rows), jnp.bfloat16),
            pltpu.VMEM((units, 16, rows), jnp.float32),
            pltpu.VMEM((units, 16, rows), jnp.bfloat16),
            pltpu.VMEM((units, 16, rows), jnp.bfloat16),
            pltpu.VMEM((2, units * UNIT, rows), jnp.float32),
            pltpu.SemaphoreType.DMA((4,)),
            pltpu.SemaphoreType.DMA((n_copies,)),
            pltpu.SemaphoreType.DMA((n_copies,)),
            pltpu.SemaphoreType.DMA((len(PANELS) * 8,)),
            pltpu.SemaphoreType.DMA((len(PANELS) * 8,)),
        ],
        compiler_params=pltpu.CompilerParams(
            collective_id=0, has_side_effects=True, vmem_limit_bytes=62 * 2**20
        ),
        name="squared",
    )(s_matrix, slab, beam_hkl)
    return jnp.swapaxes(out, 1, 2)


def solution(mesh):
    placed = (P(None, "row", "col"), P(None, ("col", "row"), None), P(None, ("col", "row")))
    return jax.shard_map(
        per_device, mesh=mesh, in_specs=placed, out_specs=P(None, "row", "col"), check_vma=False
    )
```

time: 167 us -> 53.1 us (0.32)
  the two profiles are of different devices: /device:TPU:4 before, /device:TPU:1 now
where the time goes in v2:
time: 53.1 us; the launch traced here: 52.8 us
  Pallas kernels  51.3 us (97%)
  local copies, waits for them, and re-layouts  1.54 us (3%)
    pallas_call x1, Pallas kernels, per_device(): pl.pallas_call(kernel, out_shape=jax.ShapeDtypeStruct((2, units * UNIT, r...  51.3 us
    unnamed x1, local copies, waits for them, and re-layouts  1.54 us

profile of v2, /device:TPU:1, one launch (start us, length us, event | category | flops | bytes accessed | tf_op | source)
XLA Modules:
  0.0 52.8 jit_solution(10417350520076308465)
XLA Ops:
  0.0 51.3 %squared.1 = bf16[2,48,512]{2,1,0:T(8,128)(2,1)} custom-call(bf16[2,512,4096]{2,1,0:T(8,128)(2,1)} %s_any.1, bf16[2,128,384]{2,1,0:T(8,128)(2,1)} %slab_any.1, s32[3,128]{1,0:T(4,128)} %hkl_any.1), custom_call_target="tpu_custom_call" | custom-call | tf_op jit(solution)/shard_map/squared/pallas_call | solution.py:333
  51.3 1.5 %copy.5 = bf16[2,512,48]{1,2,0:T(8,128)(2,1)} copy(bf16[2,512,48]{1,2,0:T(8,128)(2,1)} %bitcast.1) | data formatting | bytes 196608

commit v3 on v0

v3 whole, which is shorter than its diff:
```python
import jax
import jax.numpy as jnp
from jax import lax
from jax.experimental import pallas as pl
from jax.experimental.pallas import tpu as pltpu
from jax.sharding import PartitionSpec as P

MESH = pl.DeviceIdType.MESH
UNIT = 8
UNITS = 2
PANELS = 3
DIRECT = PANELS - 1
OFFSETS = (0, 1, -1, 2, -2, 3, -3, 4)
SIZE = (1, 2, 2, 2, 1)
OVER_Z = ({2: 1.0, 3: 0.5},) * PANELS
RANK = None

WIRE, CORE_WIRE, Y_WIRE = 0.69 * UNITS, 0.1 * UNITS, 1.375 * UNITS
LATENCY = {"z": 1.75, "x": 2.5, "c": 1.0}
BACKLOG = 0.5
LARGEST = 2


def transfers():
    table = []
    for p in range(PANELS):
        for e in (1, 2, 3, 4):
            table.append(("z", (p, 0, e, "z"), (p, 0, e - 1)))
        for e in range(5):
            share = OVER_Z[p].get(e, 0.0)
            if share > 0:
                table.append(("z", (p, 1, e, "z"), (p, 1, e - 1)))
            if share < 1:
                table.append(("x", (p, 1, e, "x"), (p, 0, e)))
        for h in (0, 1):
            for e in range(5):
                table.append(("c", (p, h, e, "c"), (p, h, e)))
    return table


def units_of(target):
    p, h, e, link = target
    if link == "c":
        return SIZE[e] * UNITS
    share = OVER_Z[p].get(e, 0.0) if h else 1.0
    if link == "z":
        return int(UNITS * share) if e < 4 else UNITS // 2
    return int(SIZE[e] * UNITS * (1 - share))


def schedule(table):
    targets = {t[1] for t in table}

    def parts(key):
        return [key + (link,) for link in ("z", "x") if key + (link,) in targets]

    def depth(key):
        return 1 + max([depth(t[1][:3]) for t in table if t[0] != "c" and t[2] == key], default=0)

    if RANK is None:
        rank = {t[1]: t[1][0] * 100 - (0 if t[0] == "c" else 10 * depth(t[1][:3])) for t in table}
    else:
        rank = {t[1]: r for t, r in zip(table, RANK)}
    waiting = {link: sorted((t for t in table if t[0] == link), key=lambda t: rank[t[1]]) for link in LATENCY}
    blocks = [(p, h, e) for p in range(PANELS) for e in range(5) for h in (0, 1)]
    free = {"z": 0.0, "x": 0.0, "c": 0.0, "y": 0.0}
    arrive, later, order, now = {}, [], [], 0.0
    while any(waiting.values()) or blocks or later:
        moved = False
        for link in waiting:
            if link != "c" and free[link] - now >= BACKLOG:
                continue
            for t in waiting[link]:
                if all(arrive.get(k, 1e9) <= now for k in parts(t[2])):
                    wire = units_of(t[1]) / UNITS * (CORE_WIRE if link == "c" else WIRE)
                    free[link] = max(free[link], now) + wire
                    arrive[t[1]] = free[link] + LATENCY[link]
                    order.append(("send", t))
                    waiting[link].remove(t)
                    now += 0.08 if link == "z" else 0.04
                    moved = True
                    break
        if moved:
            continue
        if later and later[0][0] <= now:
            _, op, p = later.pop(0)
            order.append((op, p))
            now += 0.05 * UNITS
            if op == "scatter_x":
                free["x"] = max(free["x"], now) + 0.35 * UNITS
                later.append((free["x"] + 1.9, "finish", p))
                later.sort()
            continue
        ready = [
            b for b in blocks if all(arrive.get(k, 1e9) <= now for k in parts(b)) and arrive.get(b + ("c",), 1e9) <= now
        ]
        if ready:
            p, n, job = min(b[0] for b in ready), 0, []
            for b in ready:
                if b[0] == p and (not job or n + SIZE[b[2]] <= LARGEST):
                    job.append(b)
                    n += SIZE[b[2]]
            for b in job:
                blocks.remove(b)
            last = all(b[0] != p for b in blocks)
            order.append(("product", p, tuple(b[1:] for b in job), last))
            now += 0.03 + 0.165 * n
            if last:
                now += 0.1 * UNITS
                order.append(("scatter", p))
                free["y"] = max(free["y"], now) + Y_WIRE
                if p == DIRECT:
                    free["x"] = max(free["x"], now) + Y_WIRE
                    later.append((max(free["y"] + 2.4, free["x"] + 2.9), "finish", p))
                else:
                    later.append((free["y"] + 2.2, "scatter_x", p))
                later.sort()
            continue
        events = list(arrive.values()) + [t[0] for t in later]
        events += [free[link] - BACKLOG + 1e-6 for link in ("z", "x") if waiting[link]]
        now = min(t for t in events if t > now)
    return order


def kernel(s_any, slab_any, hkl_any, out_ref, s_ref, slab_ref, hkl_ref, turned, got, acc, total, part, yrecv, drecv,
           ysum, xsend, xrecv, final, in_sem, send_sem, recv_sem, rs_send, rs_recv):
    row = lax.axis_index("row")
    col = lax.axis_index("col")
    z, xh, core = row // 4, (row // 2) % 2, row % 2
    y, xl = col // 2, col % 2
    rows = s_any.shape[1]
    peer = {
        "zp": ((z + 1) % 8 * 4 + xh * 2 + core, col),
        "zm": ((z + 7) % 8 * 4 + xh * 2 + core, col),
        "x": (z * 4 + (1 - xh) * 2 + core, col),
        "c": (z * 4 + xh * 2 + 1 - core, col),
    }
    owner = {(dy, dx): (y + dy) % 4 * 2 + (xl + dx) % 2 for dy in range(4) for dx in range(2) if dy or dx}
    owners = list(owner)
    for k in owner:
        peer[k] = (row, owner[k])

    slab_copy = pltpu.make_async_copy(slab_any, slab_ref, in_sem.at[0])
    hkl_copy = pltpu.make_async_copy(hkl_any, hkl_ref, in_sem.at[1])
    s_copies = [
        pltpu.make_async_copy(s_any.at[i], s_ref.at[pl.ds(i * rows, rows)], in_sem.at[2 + i]) for i in range(2)
    ]
    slab_copy.start()
    hkl_copy.start()
    barrier = pltpu.get_barrier_semaphore()
    for name in peer:
        pl.semaphore_signal(barrier, inc=1, device_id=peer[name], device_id_type=MESH)

    hkl_copy.wait()
    f = hkl_ref[...].astype(jnp.float32)
    h0, h1, h2 = f[0:1], f[1:2], f[2:3]
    angles = 0.61 * (h0 * h0 + h1 * h1 + h2 * h2) + 0.29 * h0 - 0.17 * h1 + 0.43 * h2
    cosine, sine = jnp.cos(angles), jnp.sin(angles)
    slab_copy.wait()
    for c in s_copies:
        c.start()
    for i in range(2):
        turned[i] = jnp.transpose(slab_ref[i].astype(jnp.float32))

    def slot(p, h, d, mine):
        return (p * 32 + mine * 16 + h * 8 + OFFSETS.index(d)) * UNITS

    def group(p, h, e, mine):
        return got.at[pl.ds(slot(p, h, e, mine), SIZE[e] * UNITS)]

    def phase(p):
        for u in range(UNITS):
            for o in range(8):
                at = 48 * o + UNIT * (p * UNITS + u)
                re, im = turned[0, at:at + UNIT], turned[1, at:at + UNIT]
                both = jnp.concatenate([cosine * re - sine * im, cosine * im + sine * re], axis=0)
                got[slot(p, 0, 0, 0) + u, 16 * o:16 * o + 16] = both.astype(jnp.bfloat16)

    table = transfers()
    signals = []
    for link, dst, _ in table:
        key = dst[:3] + (link == "c",)
        if key not in signals:
            signals.append(key)

    def move(p, at, to, size, link, key):
        return pltpu.make_async_remote_copy(
            src_ref=got.at[pl.ds(at, size)], dst_ref=got.at[pl.ds(to, size)],
            send_sem=send_sem.at[p], recv_sem=recv_sem.at[signals.index(key)],
            device_id=peer[link], device_id_type=MESH,
        )

    def moves(link, dst, src):
        p, h, e, _ = dst
        key = (p, h, e, link == "c")
        size = units_of(dst)
        if link == "c":
            return [move(p, slot(p, h, e, 0), slot(p, h, e, 1), size, "c", key)]
        if link == "x":
            skip = (SIZE[e] * UNITS - size) // 2
            return [move(p, slot(p, 0, e, 0) + skip, slot(p, 1, e, 0) + skip, size, "x", key)]
        both = []
        for s, way in ((1, "zm"), (-1, "zp")):
            skip = 0 if s == 1 else UNITS - size
            at = slot(p, h, s * (e - 1), 0) + skip
            to = slot(p, h, s * e if e < 4 else 4, 0) + skip
            both.append(move(p, at, to, size, way, key))
        return both

    seen = set()

    def need(p, h, e, twin):
        key = (p, h, e, twin)
        if key in seen:
            return
        seen.add(key)
        if key[1:] == (0, 0, False):
            phase(p)
            return
        ref = group(p, h, e, 1 if twin else 0)
        pltpu.make_async_remote_copy(
            src_ref=ref, dst_ref=ref, send_sem=send_sem.at[p], recv_sem=recv_sem.at[signals.index(key)],
            device_id=peer["c"], device_id_type=MESH,
        ).wait_recv()

    begun = set()

    def product(p, job, last):
        left, right = [], []
        for h, e in job:
            for d in (e, -e) if e in (1, 2, 3) else (e,):
                for mine in (0, 1):
                    left.append(got[pl.ds(slot(p, h, d, mine), UNITS)].reshape(UNITS * 128, 128))
                    chip = (z + d + 8) % 8 * 2 + (xh if h == 0 else 1 - xh)
                    beam = chip * 2 + (core if mine == 0 else 1 - core)
                    right.append(s_ref[:, pl.ds(pl.multiple_of(beam * 128, 128), 128)])
        result = lax.dot_general(
            jnp.concatenate(left, axis=1), jnp.concatenate(right, axis=1), (((1,), (1,)), ((), ())),
            preferred_element_type=jnp.float32,
        )
        if p in begun:
            result += acc[p]
        begun.add(p)
        if not last:
            acc[p] = result
            return
        pairs = result.reshape(UNITS * 8, 2, UNIT, 2 * rows)
        re, im = pairs[:, 0], pairs[:, 1]
        both = jnp.stack([re[..., :rows] - im[..., rows:], im[..., :rows] + re[..., rows:]], axis=1)
        both = both.reshape(UNITS, 128, rows)
        total[p] = both
        part[p] = both.astype(jnp.bfloat16)

    def y_copy(p, j):
        to = pl.ds(pl.multiple_of((y + j) % 4 * 32, 32), 32)
        return pltpu.make_async_remote_copy(
            src_ref=part.at[p, :, to], dst_ref=yrecv.at[p, j - 1],
            send_sem=rs_send.at[p], recv_sem=rs_recv.at[p], device_id=peer[(j, 0)], device_id_type=MESH,
        )

    def x_copy(p):
        return pltpu.make_async_remote_copy(
            src_ref=xsend.at[p], dst_ref=xrecv.at[p], send_sem=rs_send.at[PANELS + p], recv_sem=rs_recv.at[PANELS + p],
            device_id=peer[(0, 1)], device_id_type=MESH,
        )

    def direct_copy(p, k):
        to = pl.ds(pl.multiple_of(owner[k] * 16, 16), 16)
        return pltpu.make_async_remote_copy(
            src_ref=part.at[p, :, to], dst_ref=drecv.at[owners.index(k)],
            send_sem=rs_send.at[p], recv_sem=rs_recv.at[p], device_id=peer[k], device_id_type=MESH,
        )

    def scattered(p):
        ref = drecv if p == DIRECT else yrecv.at[p]
        return pltpu.make_async_remote_copy(
            src_ref=ref, dst_ref=ref, send_sem=rs_send.at[p], recv_sem=rs_recv.at[p],
            device_id=peer["c"], device_id_type=MESH,
        )

    def scatter(p):
        if p == DIRECT:
            for k in ((2, 1), (2, 0), (1, 1), (3, 1), (1, 0), (3, 0), (0, 1)):
                direct_copy(p, k).start()
        else:
            for j in (2, 1, 3):
                y_copy(p, j).start()

    def scatter_x(p):
        scattered(p).wait_recv()
        for to in (1, 0):
            which = (xl + to) % 2
            t = total[p, :, pl.ds(pl.multiple_of(y * 32 + which * 16, 16), 16)]
            for j in range(3):
                t += yrecv[p, j, :, pl.ds(pl.multiple_of(which * 16, 16), 16)].astype(jnp.float32)
            if to:
                xsend[p] = t.astype(jnp.bfloat16)
                x_copy(p).start()
            else:
                ysum[p] = t

    def finish(p):
        if p == DIRECT:
            scattered(p).wait_recv()
            t = total[p, :, pl.ds(pl.multiple_of(col * 16, 16), 16)]
            for i in range(len(owners)):
                t += drecv[i].astype(jnp.float32)
        else:
            x_copy(p).wait_recv()
            t = ysum[p] + xrecv[p].astype(jnp.float32)
        for u in range(UNITS):
            at = UNIT * (p * UNITS + u)
            final[0, at:at + UNIT] = t[u, :UNIT]
            final[1, at:at + UNIT] = t[u, UNIT:]

    need(0, 0, 0, False)
    pl.semaphore_wait(barrier, len(peer))
    order = schedule(table)
    drained = max(i for i, step in enumerate(order) if step[0] == "scatter")
    loaded = False
    for i, step in enumerate(order):
        if step[0] == "send":
            link, dst, src = step[1]
            need(*src, False)
            for c in moves(link, dst, src):
                c.start()
        elif step[0] == "product":
            _, p, job, last = step
            for h, e in job:
                need(p, h, e, False)
                need(p, h, e, True)
            if not loaded:
                loaded = True
                for c in s_copies:
                    c.wait()
            product(p, job, last)
        else:
            {"scatter": scatter, "scatter_x": scatter_x, "finish": finish}[step[0]](step[1])
        if i == drained:
            for p in range(PANELS):
                sent = sum(units_of(t[1]) * (2 if t[0] == "z" else 1) for t in table if t[1][0] == p)
                move(p, 0, 0, sent, "c", signals[0]).wait_send()
    out_ref[...] = final[...].astype(jnp.bfloat16)
    for p in range(PANELS):
        scattered(p).wait_send()
        if p != DIRECT:
            x_copy(p).wait_send()


def per_device(s_matrix, slab, beam_hkl):
    rows, beams = s_matrix.shape[1:]
    units = PANELS * UNITS
    n_signals = PANELS * 19
    out = pl.pallas_call(
        kernel,
        out_shape=pltpu.VMEM((2, units * UNIT, rows), jnp.bfloat16),
        in_specs=[pl.BlockSpec(memory_space=pltpu.HBM)] * 3,
        out_specs=pl.BlockSpec(memory_space=pltpu.VMEM),
        scratch_shapes=[
            pltpu.VMEM((2 * rows, beams), jnp.bfloat16),
            pltpu.VMEM(slab.shape, jnp.bfloat16),
            pltpu.VMEM(beam_hkl.shape, jnp.int32),
            pltpu.VMEM((2, slab.shape[2], slab.shape[1]), jnp.float32),
            pltpu.VMEM((units * 32, 128, 128), jnp.bfloat16),
            pltpu.VMEM((PANELS, UNITS * 128, 2 * rows), jnp.float32),
            pltpu.VMEM((PANELS, UNITS, 128, rows), jnp.float32),
            pltpu.VMEM((PANELS, UNITS, 128, rows), jnp.bfloat16),
            pltpu.VMEM((PANELS, 3, UNITS, 32, rows), jnp.bfloat16),
            pltpu.VMEM((7, UNITS, 16, rows), jnp.bfloat16),
            pltpu.VMEM((PANELS, UNITS, 16, rows), jnp.float32),
            pltpu.VMEM((PANELS, UNITS, 16, rows), jnp.bfloat16),
            pltpu.VMEM((PANELS, UNITS, 16, rows), jnp.bfloat16),
            pltpu.VMEM((2, units * UNIT, rows), jnp.float32),
            pltpu.SemaphoreType.DMA((4,)),
            pltpu.SemaphoreType.DMA((PANELS,)),
            pltpu.SemaphoreType.DMA((n_signals,)),
            pltpu.SemaphoreType.DMA((2 * PANELS,)),
            pltpu.SemaphoreType.DMA((2 * PANELS,)),
        ],
        compiler_params=pltpu.CompilerParams(
            collective_id=0, has_side_effects=True, vmem_limit_bytes=63 * 2**20
        ),
        name="squared",
    )(s_matrix, slab, beam_hkl)
    return jnp.swapaxes(out, 1, 2)


def solution(mesh):
    placed = (P(None, "row", "col"), P(None, ("col", "row"), None), P(None, ("col", "row")))
    return jax.shard_map(
        per_device, mesh=mesh, in_specs=placed, out_specs=P(None, "row", "col"), check_vma=False
    )
```

time: 167 us -> 47 us (0.28)
  the two profiles are of different devices: /device:TPU:4 before, /device:TPU:1 now
where the time goes in v3:
time: 47 us; the launch traced here: 46.9 us
  Pallas kernels  46.3 us (99%)
  local copies, waits for them, and re-layouts  0.64 us (1%)
    pallas_call x1, Pallas kernels, per_device(): pl.pallas_call(kernel, out_shape=pltpu.VMEM((2, units * UNIT, rows), jnp....  46.3 us

profile of v3, /device:TPU:1, one launch (start us, length us, event | category | flops | bytes accessed | tf_op | source)
XLA Modules:
  0.0 46.9 jit_solution(14377443777467240136)
XLA Ops:
  0.0 46.3 %squared.1 = bf16[2,48,512]{2,1,0:T(8,128)(2,1)S(1)} custom-call(bf16[2,512,4096]{2,1,0:T(8,128)(2,1)} %s_any.1, bf16[2,128,384]{2,1,0:T(8,128)(2,1)} %slab_any.1, s32[3,128]{1,0:T(4,128)} %hkl_any.1), custom_call_target="tpu_custom_call" | custom-call | tf_op jit(solution)/shard_map/squared/pallas_call | solution.py:354
  46.3 0.6 %copy.5 = bf16[2,512,48]{1,2,0:T(8,128)(2,1)} copy(bf16[2,512,48]{1,2,0:T(8,128)(2,1)S(1)} %bitcast.1) | data formatting | bytes 196608

commit v4 on v3

--- a/solution.py
+++ b/solution.py
@@ -9,16 +9,21 @@
 UNIT = 8
 UNITS = 2
 PANELS = 3
-DIRECT = PANELS - 1
+DIRECT = (1, 2)
 OFFSETS = (0, 1, -1, 2, -2, 3, -3, 4)
 SIZE = (1, 2, 2, 2, 1)
-OVER_Z = ({2: 1.0, 3: 0.5},) * PANELS
-RANK = None
+OVER_Z = ({2: 1.0, 3: 0.5}, {1: 1.0, 3: 0.5}, {2: 1.0, 3: 0.5})
+RANK = (
+    -3174, -2803, -1957, -5707, 128, 2109, 1428, -980, -364, 1850, 410, 460, -1562, -3876, -3764, -1949,
+    -605, 570, 1667, 718, 3137, 1407, -1062, 1151, 3079, 2229, -1576, 2413, 2506, -2405, 335, 258,
+    -16, 4147, 315, -1335, 3264, 1811, -989, 908, 3207, -30, 1700, 349, 195, 933, 1704, 429,
+    1786, 758, 2040, 3883, 1399, 17, 1124, 1720, -634, 2325, 3003, 3400,
+)
 
 WIRE, CORE_WIRE, Y_WIRE = 0.69 * UNITS, 0.1 * UNITS, 1.375 * UNITS
-LATENCY = {"z": 1.75, "x": 2.5, "c": 1.0}
+LATENCY = {"z": 2.1, "x": 2.7, "c": 0.9}
 BACKLOG = 0.5
-LARGEST = 2
+LARGEST = 4
 
 
 def transfers():
@@ -54,13 +59,7 @@
     def parts(key):
         return [key + (link,) for link in ("z", "x") if key + (link,) in targets]
 
-    def depth(key):
-        return 1 + max([depth(t[1][:3]) for t in table if t[0] != "c" and t[2] == key], default=0)
-
-    if RANK is None:
-        rank = {t[1]: t[1][0] * 100 - (0 if t[0] == "c" else 10 * depth(t[1][:3])) for t in table}
-    else:
-        rank = {t[1]: r for t, r in zip(table, RANK)}
+    rank = {t[1]: r for t, r in zip(table, RANK)}
     waiting = {link: sorted((t for t in table if t[0] == link), key=lambda t: rank[t[1]]) for link in LATENCY}
     blocks = [(p, h, e) for p in range(PANELS) for e in range(5) for h in (0, 1)]
     free = {"z": 0.0, "x": 0.0, "c": 0.0, "y": 0.0}
@@ -84,7 +83,8 @@
             continue
         if later and later[0][0] <= now:
             _, op, p = later.pop(0)
-            order.append((op, p))
+            if op == "scatter_x":
+                order.append((op, p))
             now += 0.05 * UNITS
             if op == "scatter_x":
                 free["x"] = max(free["x"], now) + 0.35 * UNITS
@@ -97,19 +97,20 @@
         if ready:
             p, n, job = min(b[0] for b in ready), 0, []
             for b in ready:
-                if b[0] == p and (not job or n + SIZE[b[2]] <= LARGEST):
-                    job.append(b)
-                    n += SIZE[b[2]]
+                if b[0] != p or (job and n + SIZE[b[2]] > LARGEST):
+                    break
+                job.append(b)
+                n += SIZE[b[2]]
             for b in job:
                 blocks.remove(b)
             last = all(b[0] != p for b in blocks)
             order.append(("product", p, tuple(b[1:] for b in job), last))
             now += 0.03 + 0.165 * n
             if last:
-                now += 0.1 * UNITS
+                now += 0.21
                 order.append(("scatter", p))
                 free["y"] = max(free["y"], now) + Y_WIRE
-                if p == DIRECT:
+                if p in DIRECT:
                     free["x"] = max(free["x"], now) + Y_WIRE
                     later.append((max(free["y"] + 2.4, free["x"] + 2.9), "finish", p))
                 else:
@@ -267,19 +268,19 @@
     def direct_copy(p, k):
         to = pl.ds(pl.multiple_of(owner[k] * 16, 16), 16)
         return pltpu.make_async_remote_copy(
-            src_ref=part.at[p, :, to], dst_ref=drecv.at[owners.index(k)],
+            src_ref=part.at[p, :, to], dst_ref=drecv.at[p, owners.index(k)],
             send_sem=rs_send.at[p], recv_sem=rs_recv.at[p], device_id=peer[k], device_id_type=MESH,
         )
 
     def scattered(p):
-        ref = drecv if p == DIRECT else yrecv.at[p]
+        ref = drecv.at[p] if p in DIRECT else yrecv.at[p]
         return pltpu.make_async_remote_copy(
             src_ref=ref, dst_ref=ref, send_sem=rs_send.at[p], recv_sem=rs_recv.at[p],
             device_id=peer["c"], device_id_type=MESH,
         )
 
     def scatter(p):
-        if p == DIRECT:
+        if p in DIRECT:
             for k in ((2, 1), (2, 0), (1, 1), (3, 1), (1, 0), (3, 0), (0, 1)):
                 direct_copy(p, k).start()
         else:
@@ -300,11 +301,11 @@
                 ysum[p] = t
 
     def finish(p):
-        if p == DIRECT:
+        if p in DIRECT:
             scattered(p).wait_recv()
             t = total[p, :, pl.ds(pl.multiple_of(col * 16, 16), 16)]
             for i in range(len(owners)):
-                t += drecv[i].astype(jnp.float32)
+                t += drecv[p, i].astype(jnp.float32)
         else:
             x_copy(p).wait_recv()
             t = ysum[p] + xrecv[p].astype(jnp.float32)
@@ -335,15 +336,17 @@
                     c.wait()
             product(p, job, last)
         else:
-            {"scatter": scatter, "scatter_x": scatter_x, "finish": finish}[step[0]](step[1])
+            {"scatter": scatter, "scatter_x": scatter_x}[step[0]](step[1])
         if i == drained:
             for p in range(PANELS):
                 sent = sum(units_of(t[1]) * (2 if t[0] == "z" else 1) for t in table if t[1][0] == p)
                 move(p, 0, 0, sent, "c", signals[0]).wait_send()
+    for p in range(PANELS):
+        finish(p)
     out_ref[...] = final[...].astype(jnp.bfloat16)
     for p in range(PANELS):
         scattered(p).wait_send()
-        if p != DIRECT:
+        if p not in DIRECT:
             x_copy(p).wait_send()
 
 
@@ -366,7 +369,7 @@
             pltpu.VMEM((PANELS, UNITS, 128, rows), jnp.float32),
             pltpu.VMEM((PANELS, UNITS, 128, rows), jnp.bfloat16),
             pltpu.VMEM((PANELS, 3, UNITS, 32, rows), jnp.bfloat16),
-            pltpu.VMEM((7, UNITS, 16, rows), jnp.bfloat16),
+            pltpu.VMEM((PANELS, 7, UNITS, 16, rows), jnp.bfloat16),
             pltpu.VMEM((PANELS, UNITS, 16, rows), jnp.float32),
             pltpu.VMEM((PANELS, UNITS, 16, rows), jnp.bfloat16),
             pltpu.VMEM((PANELS, UNITS, 16, rows), jnp.bfloat16),

time: 47 us -> 45.1 us (0.960)
  Pallas kernels: 46.3 us -> 44.3 us
    pallas_call x1, Pallas kernels: 46.3 us -> 44.3 us  [per_device(): pl.pallas_call(kernel, out_shape=pltpu.VMEM((2, units * UNIT, rows), jnp....]
where the time goes in v4:
time: 45.1 us; the launch traced here: 45 us
  Pallas kernels  44.3 us (98%)
  local copies, waits for them, and re-layouts  0.64 us (1%)
    pallas_call x1, Pallas kernels, per_device(): pl.pallas_call(kernel, out_shape=pltpu.VMEM((2, units * UNIT, rows), jnp....  44.3 us

profile of v4, /device:TPU:1, one launch (start us, length us, event | category | flops | bytes accessed | tf_op | source)
XLA Modules:
  0.0 45.0 jit_solution(10522720640617733179)
XLA Ops:
  0.0 44.3 %squared.1 = bf16[2,48,512]{2,1,0:T(8,128)(2,1)S(1)} custom-call(bf16[2,512,4096]{2,1,0:T(8,128)(2,1)} %s_any.1, bf16[2,128,384]{2,1,0:T(8,128)(2,1)} %slab_any.1, s32[3,128]{1,0:T(4,128)} %hkl_any.1), custom_call_target="tpu_custom_call" | custom-call | tf_op jit(solution)/shard_map/squared/pallas_call | solution.py:357
  44.3 0.6 %copy.5 = bf16[2,512,48]{1,2,0:T(8,128)(2,1)} copy(bf16[2,512,48]{1,2,0:T(8,128)(2,1)S(1)} %bitcast.1) | data formatting | bytes 196608

commit v5 on v4

v5 whole, which is shorter than its diff:
```python
import jax
import jax.numpy as jnp
from jax import lax
from jax.experimental import pallas as pl
from jax.experimental.pallas import tpu as pltpu
from jax.sharding import PartitionSpec as P

MESH = pl.DeviceIdType.MESH
UNIT = 8
PANELS = ((0, 1), (1, 2), (3, 2), (5, 1))
DIRECT = (2, 3)
OFFSETS = (0, 1, -1, 2, -2, 3, -3, 4)
SIZE = (1, 2, 2, 2, 1)
OVER_Z = ({2: 1.0, 4: 1.0}, {2: 1.0, 4: 1.0}, {2: 1.0, 3: 0.5}, {3: 1.0, 4: 1.0})
ORDER = (
    0, 42, 23, 28, 19, 38, 58, 5, 1, 4, 20, 10, 24, 39, 43, 2, 14, 21, 53, 68, 9, 49, 11, 15, 40, 6, 30, 29, 33, 7,
    59, 3, (0, ((1, 1), (0, 2))), 50, (0, ((0, 1),)), 26, 22, (2, ((0, 1),)), (2, ((1, 0),)), 12, (2, ((0, 2),)),
    34, 41, 44, (1, ((0, 1), (0, 0))), 31, 54, (0, ((0, 0), (0, 3))), 16, 51, 64, (1, ((1, 1),)), 8, 46, 13, 17,
    (1, ((0, 3),)), 25, (0, ((1, 2),)), (1, ((0, 2),)), 47, 48, (2, ((1, 1),)), 27, (3, ((0, 1),)), 52, 45, 62, 60,
    36, (0, ((0, 4),)), 63, 69, 18, (1, ((1, 0),)), (0, ((1, 3),)), 65, 32, 74, 67, (2, ((0, 0),)), (2, ((0, 4),)),
    35, (0, ((1, 0),)), (0, ((1, 4),)), 37, 55, (1, ((1, 3),)), (1, ((0, 4),)), (1, ((1, 2),)), 56, (1, ((1, 4),)),
    61, 70, 57, (2, ((1, 2),)), 72, 66, 75, (2, ((1, 3), (0, 3))), (2, ((1, 4),)), (3, ((0, 2),)), 73,
    (3, ((0, 0), (1, 0), (0, 3))), 71, (3, ((1, 2),)), 76, (0,), (3, ((1, 1), (1, 3))), (3, ((0, 4),)),
    (3, ((1, 4),)), (1,),
)


def transfers():
    table = []
    for p in range(len(PANELS)):
        for e in (1, 2, 3, 4):
            table.append(("z", (p, 0, e, "z"), (p, 0, e - 1)))
        for e in range(5):
            share = OVER_Z[p].get(e, 0.0)
            if share > 0:
                table.append(("z", (p, 1, e, "z"), (p, 1, e - 1)))
            if share < 1:
                table.append(("x", (p, 1, e, "x"), (p, 0, e)))
        for h in (0, 1):
            for e in range(5):
                table.append(("c", (p, h, e, "c"), (p, h, e)))
    return table


def halves_of(target):
    p, h, e, link = target
    halves = 2 * PANELS[p][1]
    if link == "c":
        return SIZE[e] * halves
    share = OVER_Z[p].get(e, 0.0) if h else 1.0
    if link == "z":
        return int(halves * share) if e < 4 else halves // 2
    return int(SIZE[e] * halves * (1 - share))


def kernel(s_any, slab_any, hkl_any, out_ref, s_ref, slab_ref, hkl_ref, turned, got, acc, total, part, yrecv, drecv,
           ysum, xsend, xrecv, final, in_sem, send_sem, recv_sem, rs_send, rs_recv):
    row = lax.axis_index("row")
    col = lax.axis_index("col")
    z, xh, core = row // 4, (row // 2) % 2, row % 2
    y, xl = col // 2, col % 2
    rows = s_any.shape[1]
    peer = {
        "zp": ((z + 1) % 8 * 4 + xh * 2 + core, col),
        "zm": ((z + 7) % 8 * 4 + xh * 2 + core, col),
        "x": (z * 4 + (1 - xh) * 2 + core, col),
        "c": (z * 4 + xh * 2 + 1 - core, col),
    }
    owner = {(dy, dx): (y + dy) % 4 * 2 + (xl + dx) % 2 for dy in range(4) for dx in range(2) if dy or dx}
    owners = list(owner)
    for k in owner:
        peer[k] = (row, owner[k])

    slab_copy = pltpu.make_async_copy(slab_any, slab_ref, in_sem.at[0])
    hkl_copy = pltpu.make_async_copy(hkl_any, hkl_ref, in_sem.at[1])
    s_copies = [
        pltpu.make_async_copy(s_any.at[i], s_ref.at[pl.ds(i * rows, rows)], in_sem.at[2 + i]) for i in range(2)
    ]
    slab_copy.start()
    hkl_copy.start()
    barrier = pltpu.get_barrier_semaphore()
    for name in peer:
        pl.semaphore_signal(barrier, inc=1, device_id=peer[name], device_id_type=MESH)

    hkl_copy.wait()
    f = hkl_ref[...].astype(jnp.float32)
    h0, h1, h2 = f[0:1], f[1:2], f[2:3]
    angles = 0.61 * (h0 * h0 + h1 * h1 + h2 * h2) + 0.29 * h0 - 0.17 * h1 + 0.43 * h2
    cosine, sine = jnp.cos(angles), jnp.sin(angles)
    slab_copy.wait()
    for c in s_copies:
        c.start()
    for i in range(2):
        turned[i] = jnp.transpose(slab_ref[i].astype(jnp.float32))

    def slot(p, h, d, mine):
        first, units = PANELS[p]
        return 2 * (first * 32 + (mine * 16 + h * 8 + OFFSETS.index(d)) * units)

    def group(p, h, e, mine):
        return got.at[pl.ds(slot(p, h, e, mine), SIZE[e] * 2 * PANELS[p][1])]

    def phase(p):
        first, units = PANELS[p]
        for u in range(units):
            for o in range(8):
                at = 48 * o + UNIT * (first + u)
                re, im = turned[0, at:at + UNIT], turned[1, at:at + UNIT]
                both = jnp.concatenate([cosine * re - sine * im, cosine * im + sine * re], axis=0)
                got[slot(p, 0, 0, 0) + 2 * u + o // 4, o % 4 * 16:o % 4 * 16 + 16] = both.astype(jnp.bfloat16)

    table = transfers()
    signals = []
    for link, dst, _ in table:
        key = dst[:3] + (link == "c",)
        if key not in signals:
            signals.append(key)

    def move(p, at, to, size, link, key):
        return pltpu.make_async_remote_copy(
            src_ref=got.at[pl.ds(at, size)], dst_ref=got.at[pl.ds(to, size)],
            send_sem=send_sem.at[p], recv_sem=recv_sem.at[signals.index(key)],
            device_id=peer[link], device_id_type=MESH,
        )

    def moves(link, dst, src):
        p, h, e, _ = dst
        key = (p, h, e, link == "c")
        size = halves_of(dst)
        if link == "c":
            return [move(p, slot(p, h, e, 0), slot(p, h, e, 1), size, "c", key)]
        if link == "x":
            skip = (SIZE[e] * 2 * PANELS[p][1] - size) // 2
            return [move(p, slot(p, 0, e, 0) + skip, slot(p, 1, e, 0) + skip, size, "x", key)]
        both = []
        for s, way in ((1, "zm"), (-1, "zp")):
            skip = 0 if s == 1 else 2 * PANELS[p][1] - size
            at = slot(p, h, s * (e - 1), 0) + skip
            to = slot(p, h, s * e if e < 4 else 4, 0) + skip
            both.append(move(p, at, to, size, way, key))
        return both

    seen = set()

    def need(p, h, e, twin):
        key = (p, h, e, twin)
        if key in seen:
            return
        seen.add(key)
        if key[1:] == (0, 0, False):
            phase(p)
            return
        ref = group(p, h, e, 1 if twin else 0)
        pltpu.make_async_remote_copy(
            src_ref=ref, dst_ref=ref, send_sem=send_sem.at[p], recv_sem=recv_sem.at[signals.index(key)],
            device_id=peer["c"], device_id_type=MESH,
        ).wait_recv()

    def panel(p):
        return pl.ds(*PANELS[p])

    begun = set()

    def product(p, job, last):
        left, right = [], []
        first, units = PANELS[p]
        for h, e in job:
            for d in (e, -e) if e in (1, 2, 3) else (e,):
                for mine in (0, 1):
                    left.append(got[pl.ds(slot(p, h, d, mine), 2 * units)].reshape(units * 128, 128))
                    chip = (z + d + 8) % 8 * 2 + (xh if h == 0 else 1 - xh)
                    beam = chip * 2 + (core if mine == 0 else 1 - core)
                    right.append(s_ref[:, pl.ds(pl.multiple_of(beam * 128, 128), 128)])
        result = lax.dot_general(
            jnp.concatenate(left, axis=1), jnp.concatenate(right, axis=1), (((1,), (1,)), ((), ())),
            preferred_element_type=jnp.float32,
        )
        mine = pl.ds(first * 128, units * 128)
        if p in begun:
            result += acc[mine]
        begun.add(p)
        if not last:
            acc[mine] = result
            return
        pairs = result.reshape(units * 8, 2, UNIT, 2 * rows)
        re, im = pairs[:, 0], pairs[:, 1]
        both = jnp.stack([re[..., :rows] - im[..., rows:], im[..., :rows] + re[..., rows:]], axis=1)
        both = both.reshape(units, 128, rows)
        total[panel(p)] = both
        part[panel(p)] = both.astype(jnp.bfloat16)

    def y_copy(p, j):
        to = pl.ds(pl.multiple_of((y + j) % 4 * 32, 32), 32)
        return pltpu.make_async_remote_copy(
            src_ref=part.at[panel(p), to], dst_ref=yrecv.at[j - 1, panel(p)],
            send_sem=rs_send.at[p], recv_sem=rs_recv.at[p], device_id=peer[(j, 0)], device_id_type=MESH,
        )

    def x_copy(p):
        return pltpu.make_async_remote_copy(
            src_ref=xsend.at[panel(p)], dst_ref=xrecv.at[panel(p)],
            send_sem=rs_send.at[len(PANELS) + p], recv_sem=rs_recv.at[len(PANELS) + p],
            device_id=peer[(0, 1)], device_id_type=MESH,
        )

    def direct_copy(p, k):
        to = pl.ds(pl.multiple_of(owner[k] * 16, 16), 16)
        return pltpu.make_async_remote_copy(
            src_ref=part.at[panel(p), to], dst_ref=drecv.at[owners.index(k), panel(p)],
            send_sem=rs_send.at[p], recv_sem=rs_recv.at[p], device_id=peer[k], device_id_type=MESH,
        )

    def scattered(p):
        ref = (drecv if p in DIRECT else yrecv).at[:, panel(p)]
        return pltpu.make_async_remote_copy(
            src_ref=ref, dst_ref=ref, send_sem=rs_send.at[p], recv_sem=rs_recv.at[p],
            device_id=peer["c"], device_id_type=MESH,
        )

    def scatter(p):
        if p in DIRECT:
            for k in ((2, 1), (2, 0), (1, 1), (3, 1), (1, 0), (3, 0), (0, 1)):
                direct_copy(p, k).start()
        else:
            for j in (2, 1, 3):
                y_copy(p, j).start()

    def scatter_x(p):
        scattered(p).wait_recv()
        for to in (1, 0):
            which = (xl + to) % 2
            t = total[panel(p), pl.ds(pl.multiple_of(y * 32 + which * 16, 16), 16)]
            for j in range(3):
                t += yrecv[j, panel(p), pl.ds(pl.multiple_of(which * 16, 16), 16)].astype(jnp.float32)
            if to:
                xsend[panel(p)] = t.astype(jnp.bfloat16)
                x_copy(p).start()
            else:
                ysum[panel(p)] = t

    def finish(p):
        if p in DIRECT:
            scattered(p).wait_recv()
            t = total[panel(p), pl.ds(pl.multiple_of(col * 16, 16), 16)]
            for i in range(len(owners)):
                t += drecv[i, panel(p)].astype(jnp.float32)
        else:
            x_copy(p).wait_recv()
            t = ysum[panel(p)] + xrecv[panel(p)].astype(jnp.float32)
        first, units = PANELS[p]
        for u in range(units):
            at = UNIT * (first + u)
            final[0, at:at + UNIT] = t[u, :UNIT]
            final[1, at:at + UNIT] = t[u, UNIT:]

    need(0, 0, 0, False)
    pl.semaphore_wait(barrier, len(peer))
    todo = {p: 10 for p in range(len(PANELS))}
    loaded = False
    for step in ORDER:
        if isinstance(step, int):
            link, dst, src = table[step]
            need(*src, False)
            for c in moves(link, dst, src):
                c.start()
        elif len(step) == 2:
            p, job = step
            for h, e in job:
                need(p, h, e, False)
                need(p, h, e, True)
            if not loaded:
                loaded = True
                for c in s_copies:
                    c.wait()
            todo[p] -= len(job)
            product(p, job, todo[p] == 0)
            if todo[p] == 0:
                scatter(p)
        else:
            scatter_x(step[0])
    for p in range(len(PANELS)):
        sent = sum(halves_of(t[1]) * (2 if t[0] == "z" else 1) for t in table if t[1][0] == p)
        move(p, 0, 0, sent, "c", signals[0]).wait_send()
    for p in range(len(PANELS)):
        finish(p)
    out_ref[...] = final[...].astype(jnp.bfloat16)
    for p in range(len(PANELS)):
        scattered(p).wait_send()
        if p not in DIRECT:
            x_copy(p).wait_send()


def per_device(s_matrix, slab, beam_hkl):
    rows, beams = s_matrix.shape[1:]
    units = sum(PANELS[-1])
    n_signals = len(PANELS) * 19
    out = pl.pallas_call(
        kernel,
        out_shape=pltpu.VMEM((2, units * UNIT, rows), jnp.bfloat16),
        in_specs=[pl.BlockSpec(memory_space=pltpu.HBM)] * 3,
        out_specs=pl.BlockSpec(memory_space=pltpu.VMEM),
        scratch_shapes=[
            pltpu.VMEM((2 * rows, beams), jnp.bfloat16),
            pltpu.VMEM(slab.shape, jnp.bfloat16),
            pltpu.VMEM(beam_hkl.shape, jnp.int32),
            pltpu.VMEM((2, slab.shape[2], slab.shape[1]), jnp.float32),
            pltpu.VMEM((units * 64, 64, 128), jnp.bfloat16),
            pltpu.VMEM((units * 128, 2 * rows), jnp.float32),
            pltpu.VMEM((units, 128, rows), jnp.float32),
            pltpu.VMEM((units, 128, rows), jnp.bfloat16),
            pltpu.VMEM((3, units, 32, rows), jnp.bfloat16),
            pltpu.VMEM((7, units, 16, rows), jnp.bfloat16),
            pltpu.VMEM((units, 16, rows), jnp.float32),
            pltpu.VMEM((units, 16, rows), jnp.bfloat16),
            pltpu.VMEM((units, 16, rows), jnp.bfloat16),
            pltpu.VMEM((2, units * UNIT, rows), jnp.float32),
            pltpu.SemaphoreType.DMA((4,)),
            pltpu.SemaphoreType.DMA((len(PANELS),)),
            pltpu.SemaphoreType.DMA((n_signals,)),
            pltpu.SemaphoreType.DMA((2 * len(PANELS),)),
            pltpu.SemaphoreType.DMA((2 * len(PANELS),)),
        ],
        compiler_params=pltpu.CompilerParams(
            collective_id=0, has_side_effects=True, vmem_limit_bytes=63 * 2**20
        ),
        name="squared",
    )(s_matrix, slab, beam_hkl)
    return jnp.swapaxes(out, 1, 2)


def solution(mesh):
    placed = (P(None, "row", "col"), P(None, ("col", "row"), None), P(None, ("col", "row")))
    return jax.shard_map(
        per_device, mesh=mesh, in_specs=placed, out_specs=P(None, "row", "col"), check_vma=False
    )
```

time: 45.1 us -> 45.1 us (level)
  no operation moved by 1% of the time
where the time goes in v5:
time: 45.1 us; the launch traced here: 45 us
  Pallas kernels  44.3 us (98%)
  local copies, waits for them, and re-layouts  0.64 us (1%)
    pallas_call x1, Pallas kernels, per_device(): pl.pallas_call(kernel, out_shape=pltpu.VMEM((2, units * UNIT, rows), jnp....  44.3 us

profile of v5, /device:TPU:1, one launch (start us, length us, event | category | flops | bytes accessed | tf_op | source)
XLA Modules:
  0.0 45.0 jit_solution(10515527509830685991)
XLA Ops:
  0.0 44.3 %squared.1 = bf16[2,48,512]{2,1,0:T(8,128)(2,1)S(1)} custom-call(bf16[2,512,4096]{2,1,0:T(8,128)(2,1)} %s_any.1, bf16[2,128,384]{2,1,0:T(8,128)(2,1)} %slab_any.1, s32[3,128]{1,0:T(4,128)} %hkl_any.1), custom_call_target="tpu_custom_call" | custom-call | tf_op jit(solution)/shard_map/squared/pallas_call | solution.py:297
  44.3 0.6 %copy.5 = bf16[2,512,48]{1,2,0:T(8,128)(2,1)} copy(bf16[2,512,48]{1,2,0:T(8,128)(2,1)S(1)} %bitcast.1) | data formatting | bytes 196608

commit v6 on v5

--- a/solution.py
+++ b/solution.py
@@ -7,21 +7,19 @@
 
 MESH = pl.DeviceIdType.MESH
 UNIT = 8
-PANELS = ((0, 1), (1, 2), (3, 2), (5, 1))
-DIRECT = (2, 3)
+PANELS = ((0, 2), (2, 2), (4, 2))
+DIRECT = (1, 2)
 OFFSETS = (0, 1, -1, 2, -2, 3, -3, 4)
 SIZE = (1, 2, 2, 2, 1)
-OVER_Z = ({2: 1.0, 4: 1.0}, {2: 1.0, 4: 1.0}, {2: 1.0, 3: 0.5}, {3: 1.0, 4: 1.0})
+OVER_Z = ({2: 1.0, 3: 0.5}, {2: 1.0, 4: 1.0}, {1: 1.0, 2: 0.5})
 ORDER = (
-    0, 42, 23, 28, 19, 38, 58, 5, 1, 4, 20, 10, 24, 39, 43, 2, 14, 21, 53, 68, 9, 49, 11, 15, 40, 6, 30, 29, 33, 7,
-    59, 3, (0, ((1, 1), (0, 2))), 50, (0, ((0, 1),)), 26, 22, (2, ((0, 1),)), (2, ((1, 0),)), 12, (2, ((0, 2),)),
-    34, 41, 44, (1, ((0, 1), (0, 0))), 31, 54, (0, ((0, 0), (0, 3))), 16, 51, 64, (1, ((1, 1),)), 8, 46, 13, 17,
-    (1, ((0, 3),)), 25, (0, ((1, 2),)), (1, ((0, 2),)), 47, 48, (2, ((1, 1),)), 27, (3, ((0, 1),)), 52, 45, 62, 60,
-    36, (0, ((0, 4),)), 63, 69, 18, (1, ((1, 0),)), (0, ((1, 3),)), 65, 32, 74, 67, (2, ((0, 0),)), (2, ((0, 4),)),
-    35, (0, ((1, 0),)), (0, ((1, 4),)), 37, 55, (1, ((1, 3),)), (1, ((0, 4),)), (1, ((1, 2),)), 56, (1, ((1, 4),)),
-    61, 70, 57, (2, ((1, 2),)), 72, 66, 75, (2, ((1, 3), (0, 3))), (2, ((1, 4),)), (3, ((0, 2),)), 73,
-    (3, ((0, 0), (1, 0), (0, 3))), 71, (3, ((1, 2),)), 76, (0,), (3, ((1, 1), (1, 3))), (3, ((0, 4),)),
-    (3, ((1, 4),)), (1,),
+    0, 24, 4, 20, 39, 5, 1, 10, 25, 21, 34, 40, 43, 11, 12, 50, 49, 2, 22, 31, 46, 6, 16, (2, ((0, 1),)), 15, 8, 3,
+    41, 27, (0, ((1, 1),)), 23, 32, (0, ((0, 1),)), 13, 29, (1, ((0, 2),)), 54, 7, (1, ((0, 3),)), 35, 30, 14, 44,
+    9, (0, ((0, 2),)), 51, (1, ((0, 0),)), 42, 26, (0, ((0, 3),)), 47, 52, (1, ((1, 1),)), (2, ((1, 0),)), 33, 17,
+    (0, ((0, 0), (1, 0))), (0, ((0, 4),)), 18, (1, ((0, 1),)), 28, (1, ((1, 0),)), 45, 19, 55, 37, 48,
+    (0, ((1, 3),)), (0, ((1, 2),)), (0, ((1, 4),)), 36, (1, ((0, 4),)), (2, ((1, 1),)), 38, (1, ((1, 3),)), 53,
+    (1, ((1, 2),)), 56, (1, ((1, 4),)), 57, (2, ((0, 2), (0, 3))), 58, (2, ((0, 4),)), (2, ((1, 2),)),
+    (2, ((1, 3), (0, 0))), (2, ((1, 4),)), (0,),
 )
 
 

time: 45.1 us -> 44.8 us (level)
  no operation moved by 1% of the time
where the time goes in v6:
time: 44.8 us; the launch traced here: 44.7 us
  Pallas kernels  44 us (98%)
  local copies, waits for them, and re-layouts  0.64 us (1%)
    pallas_call x1, Pallas kernels, per_device(): pl.pallas_call(kernel, out_shape=pltpu.VMEM((2, units * UNIT, rows), jnp....  44 us

profile of v6, /device:TPU:1, one launch (start us, length us, event | category | flops | bytes accessed | tf_op | source)
XLA Modules:
  0.0 44.7 jit_solution(6556538042541254275)
XLA Ops:
  0.0 44.0 %squared.1 = bf16[2,48,512]{2,1,0:T(8,128)(2,1)S(1)} custom-call(bf16[2,512,4096]{2,1,0:T(8,128)(2,1)} %s_any.1, bf16[2,128,384]{2,1,0:T(8,128)(2,1)} %slab_any.1, s32[3,128]{1,0:T(4,128)} %hkl_any.1), custom_call_target="tpu_custom_call" | custom-call | tf_op jit(solution)/shard_map/squared/pallas_call | solution.py:295
  44.1 0.6 %copy.5 = bf16[2,512,48]{1,2,0:T(8,128)(2,1)} copy(bf16[2,512,48]{1,2,0:T(8,128)(2,1)S(1)} %bitcast.1) | data formatting | bytes 196608

commit v7 on v5

--- a/solution.py
+++ b/solution.py
@@ -8,20 +8,19 @@
 MESH = pl.DeviceIdType.MESH
 UNIT = 8
 PANELS = ((0, 1), (1, 2), (3, 2), (5, 1))
-DIRECT = (2, 3)
+DIRECT = (1, 2, 3)
 OFFSETS = (0, 1, -1, 2, -2, 3, -3, 4)
 SIZE = (1, 2, 2, 2, 1)
 OVER_Z = ({2: 1.0, 4: 1.0}, {2: 1.0, 4: 1.0}, {2: 1.0, 3: 0.5}, {3: 1.0, 4: 1.0})
 ORDER = (
-    0, 42, 23, 28, 19, 38, 58, 5, 1, 4, 20, 10, 24, 39, 43, 2, 14, 21, 53, 68, 9, 49, 11, 15, 40, 6, 30, 29, 33, 7,
-    59, 3, (0, ((1, 1), (0, 2))), 50, (0, ((0, 1),)), 26, 22, (2, ((0, 1),)), (2, ((1, 0),)), 12, (2, ((0, 2),)),
-    34, 41, 44, (1, ((0, 1), (0, 0))), 31, 54, (0, ((0, 0), (0, 3))), 16, 51, 64, (1, ((1, 1),)), 8, 46, 13, 17,
-    (1, ((0, 3),)), 25, (0, ((1, 2),)), (1, ((0, 2),)), 47, 48, (2, ((1, 1),)), 27, (3, ((0, 1),)), 52, 45, 62, 60,
-    36, (0, ((0, 4),)), 63, 69, 18, (1, ((1, 0),)), (0, ((1, 3),)), 65, 32, 74, 67, (2, ((0, 0),)), (2, ((0, 4),)),
-    35, (0, ((1, 0),)), (0, ((1, 4),)), 37, 55, (1, ((1, 3),)), (1, ((0, 4),)), (1, ((1, 2),)), 56, (1, ((1, 4),)),
-    61, 70, 57, (2, ((1, 2),)), 72, 66, 75, (2, ((1, 3), (0, 3))), (2, ((1, 4),)), (3, ((0, 2),)), 73,
-    (3, ((0, 0), (1, 0), (0, 3))), 71, (3, ((1, 2),)), 76, (0,), (3, ((1, 1), (1, 3))), (3, ((0, 4),)),
-    (3, ((1, 4),)), (1,),
+    0, 42, 23, 28, 19, 38, 58, (1, ((0, 0),)), 5, 1, 4, 20, 10, 24, 39, 43, (0, ((0, 1),)), 2, 14, 21, 53, 68, 9,
+    49, 11, 15, (0, ((1, 0),)), (2, ((1, 0),)), 40, 6, 30, 29, 33, (0, ((0, 0),)), 7, 59, 3, (0, ((1, 1), (0, 2))),
+    50, 26, 22, (2, ((0, 1),)), 12, (1, ((1, 0),)), (2, ((0, 2),)), 34, 41, 44, (1, ((0, 1),)), 31, 54,
+    (0, ((0, 3),)), 16, 51, 64, (1, ((1, 1),)), 8, 46, 13, 17, (1, ((0, 3),)), 25, (0, ((1, 2),)), (1, ((0, 2),)),
+    47, 48, (2, ((1, 1),)), (0, ((0, 4),)), 27, (3, ((0, 1),)), 52, 45, 62, 60, 36, 63, 69, 18, (0, ((1, 3),)), 65,
+    32, 74, 67, (2, ((0, 0), (0, 4))), 35, (0, ((1, 4),)), 37, 55, (1, ((1, 3), (0, 4))), (1, ((1, 2),)), 56,
+    (1, ((1, 4),)), 61, 70, 57, (2, ((1, 2),)), 72, 66, 75, (2, ((1, 3), (0, 3))), (2, ((1, 4),)), (3, ((0, 2),)),
+    73, (3, ((0, 0), (1, 0), (0, 3))), 71, (3, ((1, 2),)), 76, (0,), (3, ((1, 1), (1, 3))), (3, ((0, 4), (1, 4))),
 )
 
 

time: 45.1 us -> 45.2 us (level)
  no operation moved by 1% of the time
where the time goes in v7:
time: 45.2 us; the launch traced here: 45.1 us
  Pallas kernels  44.5 us (98%)
  local copies, waits for them, and re-layouts  0.64 us (1%)
    pallas_call x1, Pallas kernels, per_device(): pl.pallas_call(kernel, out_shape=pltpu.VMEM((2, units * UNIT, rows), jnp....  44.5 us

profile of v7, /device:TPU:1, one launch (start us, length us, event | category | flops | bytes accessed | tf_op | source)
XLA Modules:
  0.0 45.1 jit_solution(5694213544253857471)
XLA Ops:
  0.0 44.5 %squared.1 = bf16[2,48,512]{2,1,0:T(8,128)(2,1)S(1)} custom-call(bf16[2,512,4096]{2,1,0:T(8,128)(2,1)} %s_any.1, bf16[2,128,384]{2,1,0:T(8,128)(2,1)} %slab_any.1, s32[3,128]{1,0:T(4,128)} %hkl_any.1), custom_call_target="tpu_custom_call" | custom-call | tf_op jit(solution)/shard_map/squared/pallas_call | solution.py:296
  44.5 0.6 %copy.5 = bf16[2,512,48]{1,2,0:T(8,128)(2,1)} copy(bf16[2,512,48]{1,2,0:T(8,128)(2,1)S(1)} %bitcast.1) | data formatting | bytes 196608
